TPU v7x, 256 devices: a whole 4x4x8 slice. The times are simulated.
256 devices in a mesh: row: 16 (over y, x_hi, core), col: 16 (over z, x_lo).
Axes of the slice: x: 4 (x_hi: 2, x_lo: 2; x = x_hi * 2 + x_lo), y: 4, z: 8, core: 2. Of those that a mesh axis runs over, the one named last changes fastest.
Arguments:
- cell_batch: bfloat16 [2048, 20480], P('col', 'row'), may hold values from -6 to 6
- cov_prior: bfloat16 [20480, 20480], P('row', 'col'), as said below
- omega_prior: bfloat16 [20480, 20480], P('row', 'col'), as said below
Outputs:
- cov_updated: bfloat16 [20480, 20480], P('row', 'col')
- omega_panel: bfloat16 [1024, 20480], P('col', 'row')
- column_objective: float32 [1024], P('col')
Inputs may be any that keep to these rules, and one draw needn't show every extreme that they name: `cov_prior`: Symmetric; its diagonal entries lie between 0.5 and 1.5. `omega_prior`: Symmetric; its diagonal entries lie between 1 and 4.
All inputs are finite; a program needn't handle non-finite values.
Results may differ from a plain program's by a relative error of at most 0.0047.
Values may be sent and summed in bfloat16 or wider, within the bound.
A program may use at most 128 MiB of HBM per device.

v0:
```python
import jax
import jax.numpy as jnp
from jax import lax
from jax.sharding import PartitionSpec as P

P_SIZE = 20480
PW = 64


decay_weight = 0.5
step_size = 0.2
penalty = 1.0


def broadcast(value, axis, source):
    kept = jnp.where(lax.axis_index(axis) == source, value, 0).astype(value.dtype)
    return lax.psum(kept, axis)


def contract(left_rows, right_rows):
    return lax.dot_general(
        left_rows, right_rows, (((1,), (1,)), ((), ())), preferred_element_type=jnp.float32
    )


def per_device(cell_batch, cov_prior, omega_prior):
    rows_count = lax.axis_size("row")
    cols_count = lax.axis_size("col")
    fold_ratio = rows_count // cols_count
    row_width = omega_prior.shape[0]
    col_number = lax.axis_index("col")
    row_number = lax.axis_index("row")
    own_slab = lax.all_gather(cell_batch, "col", axis=0, tiled=True)
    mirrored = broadcast(own_slab, "row", col_number * fold_ratio + 0)
    product = lax.dot_general(
        own_slab, mirrored, (((0,), (0,)), ((), ())), preferred_element_type=jnp.float32
    )
    scale_new = (1.0 - decay_weight) / own_slab.shape[0]
    cov_updated = (decay_weight * cov_prior.astype(jnp.float32) + scale_new * product).astype(
        jnp.bfloat16
    )
    cov_rows, omega_rows = (
        lax.all_gather(cov_updated[:PW], "row", axis=0, tiled=True),
        lax.all_gather(omega_prior[:PW], "row", axis=0, tiled=True),
    )
    own_rows = PW * fold_ratio
    omega_cols_half = (
        omega_prior.reshape(row_width, fold_ratio, row_width)[:, :, :PW]
        .reshape(row_width, own_rows)
        .T
    )
    omega_vals = omega_cols_half.astype(jnp.float32)
    positions = lax.iota(jnp.int32, own_rows)
    same_block = row_number == col_number * fold_ratio + positions // PW
    diagonal = same_block[:, None] & (
        (positions % PW)[:, None] == lax.iota(jnp.int32, row_width)[None, :]
    )
    own_diag = jnp.where(diagonal, omega_vals, jnp.float32(1.0))
    inverse = jnp.where(diagonal, 1.0 / own_diag, jnp.float32(0.0))
    logs = jnp.sum(jnp.where(diagonal, jnp.log(own_diag), jnp.float32(0.0)), axis=1)
    lasso = penalty * jnp.sum(jnp.where(diagonal, jnp.float32(0.0), jnp.abs(omega_vals)), axis=1)
    summed = lax.psum_scatter(
        jnp.concatenate(
            [contract(cov_rows, omega_prior), contract(omega_rows, cov_updated)], axis=1
        ),
        "col",
        scatter_dimension=0,
        tiled=True,
    )
    first_sum = summed[:, :row_width]
    second_sum = summed[:, row_width:]
    both_sum = first_sum + second_sum
    quadratic = 0.5 * jnp.sum(omega_vals * second_sum, axis=1)
    column_objective = lax.psum(quadratic + lasso - logs, "row") / P_SIZE
    gradient = 0.5 * both_sum - inverse
    stepped = omega_vals - step_size * gradient
    shrunk = jnp.sign(stepped) * jnp.maximum(jnp.abs(stepped) - step_size * penalty, 0.0)
    omega_panel = jnp.where(diagonal, stepped, shrunk).astype(jnp.bfloat16)
    return (cov_updated, omega_panel, column_objective)


def solution(mesh):
    return jax.shard_map(
        per_device,
        mesh=mesh,
        in_specs=(P("col", "row"), P("row", "col"), P("row", "col")),
        out_specs=(P("row", "col"), P("col", "row"), P("col")),
        check_vma=False,
    )
```

profile of v0, /device:TPU:32, one launch (start us, length us, event | category | flops | bytes accessed | tf_op | source)
XLA Modules:
  0.0 705.4 jit_solution(16349236336308614956)
XLA Ops:
  7.2 0.0 all-gather.4.cloned.1.call-start
  7.2 0.7 all-gather.4.cloned.1.call-update
  7.9 0.0 all-reduce.2.cloned.1.call-start
  8.0 123.7 %all-gather.4.cloned.1.call-done = bf16[2048,1280]{1,0:T(8,128)(2,1)} async-done(((bf16[128,1280]{1,0:T(8,128)(2,1)}), bf16[2048,1280]{1,0:T(8,128)(2,1)}) %all-gather.4.cloned.1.call-update) | async-done | bytes 5242896 | tf_op jit(solution)/shard_map/all_gather | solution.py:33
  131.6 2.7 broadcast_select_fusion
  134.3 0.0 all-gather.8.cloned.1.call-start
  134.4 1.9 copy-done
  136.2 0.7 slice.17
  136.9 0.0 all-gather.6.cloned.1.call-start
  137.0 167.5 %all-reduce.2.cloned.1.call-done = bf16[2048,1280]{1,0:T(8,128)(2,1)} async-done(((bf16[2048,1280]{1,0:T(8,128)(2,1)}), bf16[2048,1280]{1,0:T(8,128)(2,1)}) %all-reduce.2.cloned.1.call-update) | async-done | bytes 5242896 | tf_op jit(solution)/shard_map/psum | solution.py:17
  304.5 11.3 %fusion.2 = bf16[1280,1280]{1,0:T(8,128)(2,1)S(1)} fusion(bf16[2048,1280]{1,0:T(8,128)(2,1)} %all-reduce.2.cloned.1.call-done, bf16[2048,1280]{1,0:T(8,128)(2,1)} %all-gather.4.cloned.1.call-done, bf16[1280,1280]{1,0:T(8,128)(2,1)} %param.4), kind=kOutput, calls=%fused_computation.4 | convolution fusion | flops 6719078400 | bytes 17039360 | tf_op jit(solution)/shard_map/dot_general | solution.py:35
  315.8 1.7 copy-done.1
  317.5 0.7 slice.21
  318.2 0.0 reduce-scatter.2.cloned.1.call-start
  318.2 43.7 %all-gather.8.cloned.1.call-done = bf16[1024,1280]{1,0:T(8,128)(2,1)} async-done(((bf16[64,1280]{1,0:T(8,128)(2,1)}), bf16[1024,1280]{1,0:T(8,128)(2,1)}) %all-gather.8.cloned.1.call-update) | async-done | bytes 2621456 | tf_op jit(solution)/shard_map/all_gather | solution.py:44
  362.0 8.7 %convolution_bitcast_fusion = f32[1024,1280]{1,0:T(8,128)} fusion(bf16[1280,1280]{1,0:T(8,128)(2,1)} %copy-done.1, bf16[1024,1280]{1,0:T(8,128)(2,1)} %all-gather.8.cloned.1.call-done), kind=kOutput, calls=%fused_computation.6 | convolution fusion | flops 3355443200 | bytes 11141120 | tf_op jit(solution)/shard_map/dot_general | solution.py:21
  370.6 47.0 %all-gather.6.cloned.1.call-done = bf16[1024,1280]{1,0:T(8,128)(2,1)} async-done(((bf16[64,1280]{1,0:T(8,128)(2,1)}), bf16[1024,1280]{1,0:T(8,128)(2,1)}) %all-gather.6.cloned.1.call-update) | async-done | bytes 2621456 | tf_op jit(solution)/shard_map/all_gather | solution.py:43
  417.7 7.6 %fusion.21 = f32[1024,1280]{1,0:T(8,128)} fusion(bf16[1024,1280]{1,0:T(8,128)(2,1)} %all-gather.6.cloned.1.call-done, bf16[1280,1280]{1,0:T(8,128)(2,1)S(1)} %copy-done), kind=kOutput, calls=%fused_computation.37 | convolution fusion | flops 3355443200 | bytes 11141120 | tf_op jit(solution)/shard_map/dot_general | solution.py:21
  425.2 9.2 %pad_maximum_fusion = f32[1024,2560]{1,0:T(8,128)} fusion(f32[1024,1280]{1,0:T(8,128)} %convolution_bitcast_fusion, f32[1024,1280]{1,0:T(8,128)} %fusion.21), kind=kLoop, calls=%fused_computation | loop fusion | flops 2621440 | bytes 20971520 | tf_op jit(solution)/shard_map/concatenate | solution.py:63
  434.5 4.0 copy.6
  438.5 219.7 %reduce-scatter.2.cloned.1.call-done = f32[64,2560]{1,0:T(8,128)} async-done(((f32[1024,2560]{1,0:T(8,128)}), f32[64,2560]{1,0:T(8,128)}) %reduce-scatter.2.cloned.1.call-update) | async-done | bytes 655376 | tf_op jit(solution)/shard_map/reduce_scatter | solution.py:62
  658.3 2.3 fusion.17
  660.6 37.7 %psum.15 = f32[64]{0:T(128)S(1)} all-reduce(f32[64]{0:T(128)S(1)} %add_subtract_fusion), channel_id=1, replica_groups=mesh['row'=16,'col'=16] {'row'}, use_global_device_ids=true, to_apply=%region_5.6 | all-reduce | flops 64 | bytes 512 | tf_op jit(solution)/shard_map/psum | solution.py:74
  698.3 0.5 broadcast_multiply_fusion
  (9 shorter events, 0.1 us)
Async XLA Ops:
  7.2 124.4 %all-gather.4.cloned.1.call-start = ((), (), s32[]{:S(2)}) async-start(), calls=%async_computation.1 | async-start | bytes 5570560 | tf_op jit(solution)/shard_map/all_gather | solution.py:33
  7.9 296.6 %all-reduce.2.cloned.1.call-start = ((), (), s32[]{:S(2)}) async-start(), calls=%async_computation.2 | async-start | bytes 10485760 | tf_op jit(solution)/shard_map/psum | solution.py:17
  134.3 1.9 copy-start
  134.3 227.6 %all-gather.8.cloned.1.call-start = ((), (), s32[]{:S(2)}) async-start(), calls=%async_computation.4 | async-start | bytes 2785280 | tf_op jit(solution)/shard_map/all_gather | solution.py:44
  136.9 280.7 %all-gather.6.cloned.1.call-start = ((), (), s32[]{:S(2)}) async-start(), calls=%async_computation.3 | async-start | bytes 2785280 | tf_op jit(solution)/shard_map/all_gather | solution.py:43
  315.8 1.7 copy-start.1
  318.2 340.1 %reduce-scatter.2.cloned.1.call-start = ((), (), s32[]{:S(2)}) async-start(), calls=%async_computation.5 | async-start | bytes 11141120 | tf_op jit(solution)/shard_map/reduce_scatter | solution.py:62
Sparse Core Ops, SparseCore 0:
  9.8 121.7 all-gather.3
  134.5 169.9 all-reduce.1
  307.8 54.0 all-gather.7
  364.6 53.0 all-gather.5
  434.6 223.6 reduce-scatter.1
where the time goes:
time: 706 us; the launch traced here: 705 us
  waiting for transfers between devices  602 us (85%)
  blocking collectives  37.7 us (5%)
  matrix products  27.5 us (4%)
  other arithmetic  14.8 us (2%)
  between operations  13.8 us (2%)
  local copies, waits for them, and re-layouts  8.93 us (1%)
    reduce_scatter x1, waiting for transfers between devices, per_device(): lax.psum_scatter(jnp.concatenate([contract(cov_rows, omega_prior), contra...  220 us
    psum x1, waiting for transfers between devices, broadcast(): return lax.psum(kept, axis)  167 us
    all_gather x1, waiting for transfers between devices, per_device(): own_slab = lax.all_gather(cell_batch, 'col', axis=0, tiled=True)  124 us
    all_gather x1, waiting for transfers between devices, per_device(): lax.all_gather(cov_updated[:PW], 'row', axis=0, tiled=True)  47 us
    all_gather x1, waiting for transfers between devices, per_device(): lax.all_gather(omega_prior[:PW], 'row', axis=0, tiled=True)  43.7 us
    psum x1, blocking collectives, per_device(): column_objective = lax.psum(quadratic + lasso - logs, 'row') / P_SIZE  37.7 us
    dot_general x2, matrix products, contract(): lax.dot_general(left_rows, right_rows, (((1,), (1,)), ((), ())), preferre...  16.2 us
  transfers between devices with their start and end apart: 5, of which 5 were waited for; matrix products, arithmetic and copies ran while one was open for 4% of the time, Pallas kernels for 0%

commit v1 on v0

v1 whole, which is shorter than its diff:
```python
import functools

import jax
import jax.numpy as jnp
from jax import lax
from jax.experimental import pallas as pl
from jax.experimental.pallas import tpu as pltpu
from jax.sharding import PartitionSpec as P

P_SIZE = 20480
PW = 64

decay_weight = 0.5
step_size = 0.2
penalty = 1.0

MESH = pl.DeviceIdType.MESH
N_SEM = 192
XROWS = 64


def rows(ref, start, size, unit=16):
    if isinstance(start, int):
        return ref.at[pl.ds(start, size), :]
    return ref.at[pl.ds(pl.multiple_of(start, unit), size), :]


def nt(a, b):
    return lax.dot_general(a, b, (((1,), (1,)), ((), ())), preferred_element_type=jnp.float32)


def kernel(
    x_hbm, s_hbm, om_hbm, cov_hbm, panel_ref, obj_ref,
    xr, xc, po, pc, om, cv, acc, p1, ov, st2, rv2, st1, rv1, tot, oslots, tr,
    send_sem, recv_sem, load_sem,
):
    r = lax.axis_index("row")
    c = lax.axis_index("col")
    y, xh, core = lax.div(r, 4), lax.rem(lax.div(r, 2), 2), lax.rem(r, 2)
    z, xl = lax.div(c, 2), lax.rem(c, 2)
    width = om.shape[0]
    piece = x_hbm.shape[0]

    def rowid(yy, hh, kk):
        return lax.rem(yy + 8, 4) * 4 + hh * 2 + kk

    def colid(zz, ll):
        return lax.rem(zz + 16, 8) * 2 + ll

    d_zp, d_zm = (r, colid(z + 1, xl)), (r, colid(z - 1, xl))
    d_xl = (r, colid(z, 1 - xl))
    d_yp, d_ym = (rowid(y + 1, xh, core), c), (rowid(y - 1, xh, core), c)
    d_xh = (rowid(y, 1 - xh, core), c)
    d_core = (rowid(y, xh, 1 - core), c)
    d_tr = (c, r)

    load_x = pltpu.make_async_copy(x_hbm, rows(xr, c * piece, piece), load_sem.at[0])
    load_x.start()
    load_po = pltpu.make_async_copy(om_hbm.at[pl.ds(0, PW), :], rows(po, r * PW, PW), load_sem.at[1])
    load_po.start()
    load_om = pltpu.make_async_copy(om_hbm, om, load_sem.at[2])
    load_om.start()
    load_s = pltpu.make_async_copy(s_hbm, cv, load_sem.at[3])
    load_s.start()

    barrier = pltpu.get_barrier_semaphore()

    def greet(dev):
        pl.semaphore_signal(barrier, inc=1, device_id=dev, device_id_type=MESH)

    for i in range(1, 16):
        greet((lax.rem(r + i, 16), c))
    for dev in (d_zp, d_zm, d_xl):
        greet(dev)

    @pl.when(r != c)
    def _():
        greet(d_tr)
        pl.semaphore_wait(barrier, 19)

    @pl.when(r == c)
    def _():
        pl.semaphore_wait(barrier, 18)

    started = []
    count = [0]

    def new(n=1):
        first = count[0]
        count[0] += n
        assert count[0] <= N_SEM
        return first

    def desc(i, src, dst, dev):
        return pltpu.make_async_remote_copy(
            src_ref=src, dst_ref=dst, send_sem=send_sem.at[i], recv_sem=recv_sem.at[i],
            device_id=dev, device_id_type=MESH,
        )

    def send(i, src, dst, dev):
        d = desc(i, src, dst, dev)
        d.start()
        started.append(d)

    def arrived(i, slot):
        desc(i, slot, slot, d_core).wait_recv()

    class RowGather:
        def __init__(self, buf, m):
            self.buf, self.m, self.b = buf, m, new(19)
            self.h = m // 2

        def slot(self, yy, hh, kk, lo=0, n=None):
            return rows(self.buf, rowid(yy, hh, kk) * self.m + lo, n or self.m)

        def go(self, i, dev, yy, hh, lo=0, n=None):
            s = self.slot(yy, hh, core, lo, n)
            send(self.b + i, s, s, dev)

        def wait(self, i, yy, hh, lo=0, n=None, kk=None):
            arrived(self.b + i, self.slot(yy, hh, core if kk is None else kk, lo, n))

        def s0(self):
            self.go(0, d_xh, y, xh)
            self.go(1, d_yp, y, xh)
            self.go(2, d_ym, y, xh)
            self.go(9, d_core, y, xh)

        def s1(self):
            o = 1 - xh
            self.wait(0, y, o)
            self.go(3, d_yp, y, o)
            self.go(4, d_ym, y, o)
            self.go(10, d_core, y, o)

        def s2(self):
            h = self.h
            self.wait(1, y - 1, xh)
            self.go(5, d_yp, y - 1, xh, h, h)
            self.wait(2, y + 1, xh)
            self.go(6, d_ym, y + 1, xh, 0, h)
            self.go(11, d_core, y - 1, xh)
            self.go(12, d_core, y + 1, xh)

        def s3(self):
            h, o = self.h, 1 - xh
            self.wait(3, y - 1, o)
            self.go(7, d_yp, y - 1, o, h, h)
            self.wait(4, y + 1, o)
            self.go(8, d_ym, y + 1, o, 0, h)
            self.go(13, d_core, y - 1, o)
            self.go(14, d_core, y + 1, o)

        def s4(self):
            h, o = self.h, 1 - xh
            self.wait(5, y + 2, xh, h, h)
            self.go(15, d_core, y + 2, xh, h, h)
            self.wait(6, y + 2, xh, 0, h)
            self.go(16, d_core, y + 2, xh, 0, h)
            self.wait(7, y + 2, o, h, h)
            self.go(17, d_core, y + 2, o, h, h)
            self.wait(8, y + 2, o, 0, h)
            self.go(18, d_core, y + 2, o, 0, h)

        def s5(self):
            h, o, k = self.h, 1 - xh, 1 - core
            self.wait(9, y, xh, kk=k)
            self.wait(10, y, o, kk=k)
            self.wait(11, y - 1, xh, kk=k)
            self.wait(12, y + 1, xh, kk=k)
            self.wait(13, y - 1, o, kk=k)
            self.wait(14, y + 1, o, kk=k)
            self.wait(15, y + 2, xh, h, h, kk=k)
            self.wait(16, y + 2, xh, 0, h, kk=k)
            self.wait(17, y + 2, o, h, h, kk=k)
            self.wait(18, y + 2, o, 0, h, kk=k)

    g, gh = XROWS, XROWS // 2
    ph = piece // 2
    cg = {}

    def cid(*key):
        if key not in cg:
            cg[key] = new()
        return cg[key]

    def xs(zz, ll, lo=0, n=piece):
        return rows(xr, colid(zz, ll) * piece + lo, n)

    def csend(key, dev, zz, ll, lo=0, n=piece):
        s = xs(zz, ll, lo, n)
        send(cid(*key), s, s, dev)

    def cwait(key, zz, ll, lo=0, n=piece):
        arrived(cid(*key), xs(zz, ll, lo, n))

    rest = piece - g

    def col0():
        csend(("a",), d_xl, z, xl, 0, g)
        csend(("p+", 1), d_zp, z, xl)
        csend(("p-", 1), d_zm, z, xl)
        csend(("f", 0), d_xl, z, xl, g, rest)

    def col1():
        cwait(("a",), z, 1 - xl, 0, g)
        csend(("q+", 1), d_zp, z, 1 - xl, 0, g)
        csend(("q-", 1), d_zm, z, 1 - xl, 0, g)

    def colp(d):
        cwait(("p+", d), z - d, xl)
        if d < 3:
            csend(("p+", d + 1), d_zp, z - d, xl)
        else:
            csend(("p+", 4), d_zp, z - d, xl, 0, ph)
        csend(("f+", d), d_xl, z - d, xl, g, rest)
        cwait(("p-", d), z + d, xl)
        if d < 3:
            csend(("p-", d + 1), d_zm, z + d, xl)
        else:
            csend(("p-", 4), d_zm, z + d, xl, ph, ph)
        csend(("f-", d), d_xl, z + d, xl, g, rest)

    def colq(d):
        cwait(("q+", d), z - d, 1 - xl, 0, g)
        if d < 3:
            csend(("q+", d + 1), d_zp, z - d, 1 - xl, 0, g)
        else:
            csend(("q+", 4), d_zp, z - d, 1 - xl, 0, gh)
        cwait(("q-", d), z + d, 1 - xl, 0, g)
        if d < 3:
            csend(("q-", d + 1), d_zm, z + d, 1 - xl, 0, g)
        else:
            csend(("q-", 4), d_zm, z + d, 1 - xl, gh, gh)

    def colp4():
        cwait(("p-", 4), z + 4, xl, ph, ph)
        csend(("f", 4), d_xl, z + 4, xl, ph, ph)
        cwait(("p+", 4), z + 4, xl, 0, ph)

    def colq4():
        cwait(("q+", 4), z + 4, 1 - xl, 0, gh)
        cwait(("q-", 4), z + 4, 1 - xl, gh, gh)

    def colf(d):
        if d == 0:
            cwait(("f", 0), z, 1 - xl, g, rest)
        elif d == 4:
            cwait(("f", 4), z + 4, 1 - xl, ph, ph)
        else:
            cwait(("f+", d), z - d, 1 - xl, g, rest)
            cwait(("f-", d), z + d, 1 - xl, g, rest)

    assert g == ph

    gx = RowGather(xc, piece)
    go_ = RowGather(po, PW)
    tid = new()
    load_x.wait()
    own_x = rows(xr, c * piece, piece)

    @pl.when(r != c)
    def _():
        desc(tid, own_x, rows(xc, c * piece, piece), d_tr).start()

    @pl.when(r == c)
    def _():
        pltpu.make_async_copy(own_x, rows(xc, c * piece, piece), load_sem.at[4]).start()

    col0()
    load_po.wait()
    go_.s0()
    acc[...] = jnp.zeros_like(acc)
    col1()

    @pl.when(r != c)
    def _():
        desc(tid, own_x, rows(xc, r * piece, piece), d_tr).wait_recv()

    @pl.when(r == c)
    def _():
        pltpu.make_async_copy(own_x, rows(xc, r * piece, piece), load_sem.at[4]).wait()

    gx.s0()
    go_.s1()
    gx.s1()
    colp(1)
    go_.s2()
    colq(1)
    go_.s3()
    gx.s2()
    colp(2)
    go_.s4()
    colq(2)
    gx.s3()
    load_om.wait()
    turned = jnp.transpose(om[:, :128].astype(jnp.float32))
    ov[...] = turned[:PW, :]
    colp(3)
    gx.s4()
    colq(3)
    gx.s5()

    tile = 256

    def accumulate(lo, n):
        def body(i, carry):
            j = lax.rem(z + lo + i + 8, 8)
            k0 = pl.multiple_of(j * 2 * piece, 2 * piece)

            def inner(m, carry2):
                m0 = pl.multiple_of(m * tile, tile)
                a = xr[pl.ds(k0, 2 * piece), pl.ds(m0, tile)]
                b = xc[pl.ds(k0, 2 * piece), :]
                acc[pl.ds(m0, tile), :] += lax.dot_general(
                    a, b, (((0,), (0,)), ((), ())), preferred_element_type=jnp.float32
                )
                return carry2

            return lax.fori_loop(0, width // tile, inner, carry)

        lax.fori_loop(0, n, body, 0)

    colf(0)
    colf(1)
    colf(2)
    accumulate(-2, 5)
    colp4()
    colf(3)
    accumulate(3, 1)
    accumulate(-3, 1)
    colq4()
    colf(4)
    accumulate(4, 1)
    go_.s5()

    scale_new = (1.0 - decay_weight) / 2048
    load_s.wait()

    def finalize(lo, n):
        lo = lo if isinstance(lo, int) else pl.multiple_of(lo, 128)
        prior = cv[pl.ds(lo, n), :].astype(jnp.float32)
        cv[pl.ds(lo, n), :] = (decay_weight * prior + scale_new * acc[pl.ds(lo, n), :]).astype(jnp.bfloat16)

    finalize(0, 128)
    own_cov = pltpu.make_async_copy(cv.at[pl.ds(0, PW), :], rows(pc, r * PW, PW), load_sem.at[5])

    def fin_body(i, carry):
        finalize(128 + i * 128, 128)
        return carry

    lax.fori_loop(0, 2, fin_body, 0)
    own_cov.start()
    own_cov.wait()
    gc = RowGather(pc, PW)
    gc.s0()
    lax.fori_loop(2, width // 128 - 1, fin_body, 0)

    def product(dst, left, right):
        def body(m, carry):
            m0 = pl.multiple_of(m * tile, tile)
            dst[pl.ds(m0, tile), :] = nt(left[pl.ds(m0, tile), :], right[...])
            return carry

        lax.fori_loop(0, 16 * PW // tile, body, 0)

    class Scatter:
        def __init__(self, src, st, rv):
            self.src, self.st, self.rv = src, st, rv
            self.ids = {}
            for n, key in enumerate(
                [("+", 0, 0), ("-", 0, 1)]
                + [(d, s, h) for s in (1, 2, 3) for d in "+-" for h in (0, 1)]
                + [("x", 0, 0)]
            ):
                self.ids[key] = (n, new())

        def own(self, zz, h):
            return self.src[pl.ds(pl.multiple_of(colid(zz, h) * PW, PW), PW), :]

        def slot(self, buf, key):
            n = self.ids[key][0]
            return buf.at[pl.ds(n * PW, PW), :]

        def got(self, key):
            s = self.slot(self.rv, key)
            arrived(self.ids[key][1], s)
            return s[...].astype(jnp.float32)

        def put(self, key, value, dev):
            s = self.slot(self.st, key)
            s[...] = value.astype(jnp.bfloat16)
            send(self.ids[key][1], s, self.slot(self.rv, key), dev)

        def step(self, s):
            for d, h in ((("+"), 0), ("-", 1), ("-", 0), ("+", 1)):
                key = (d, s, h)
                if key not in self.ids:
                    continue
                zz = z + 4 - s if d == "+" else z - 4 + s
                value = self.own(zz, h)
                if (d, s - 1, h) in self.ids:
                    value = value + self.got((d, s - 1, h))
                self.put(key, value, d_zp if d == "+" else d_zm)

        def close(self):
            for h in (0, 1):
                tot[h * PW:(h + 1) * PW, :] = (
                    self.own(z, h) + self.got(("+", 3, h)) + self.got(("-", 3, h))
                )
            self.put(("x", 0, 0), tot[pl.ds(pl.multiple_of((1 - xl) * PW, PW), PW), :], d_xl)

        def result(self):
            return tot[pl.ds(pl.multiple_of(xl * PW, PW), PW), :] + self.got(("x", 0, 0))

    product(acc, po, cv)
    store_cov = pltpu.make_async_copy(cv, cov_hbm, load_sem.at[6])
    store_cov.start()
    rs2 = Scatter(acc, st2, rv2)
    rs1 = Scatter(p1, st1, rv1)
    rs2.step(0)
    gc.s1()
    rs2.step(1)
    gc.s2()
    rs2.step(2)
    gc.s3()
    rs2.step(3)
    gc.s4()
    rs2.close()
    gc.s5()

    product(p1, pc, om)
    second_sum = rs2.result()
    acc[0:PW, :] = second_sum
    rs1.step(0)
    rs1.step(1)

    omega_vals = ov[...]
    lane = lax.broadcasted_iota(jnp.int32, (PW, width), 1)
    sub = lax.broadcasted_iota(jnp.int32, (PW, width), 0)
    diagonal = (lane == sub) & (r == c)
    own_diag = jnp.where(diagonal, omega_vals, 1.0)
    terms = 0.5 * omega_vals * acc[0:PW, :] + jnp.where(
        diagonal, -jnp.log(own_diag), penalty * jnp.abs(omega_vals)
    )
    tr[...] = jnp.zeros_like(tr)
    part = terms[:, 0:128]
    for t in range(1, width // 128):
        part = part + terms[:, t * 128:(t + 1) * 128]
    tr[0:PW, :] = part
    line = jnp.sum(jnp.transpose(tr[...]), axis=0, keepdims=True)
    oslots[pl.ds(pl.multiple_of(r * 8, 8), 8), :] = jnp.broadcast_to(line, (8, 128))
    oid = new(16)

    rs1.step(2)
    mine = rows(oslots, r * 8, 8, 8)
    for i in range(1, 16):
        send(oid + i, mine, mine, (lax.rem(r + i, 16), c))
    rs1.step(3)
    rs1.close()
    for i in range(1, 16):
        arrived(oid + i, rows(oslots, lax.rem(r + 16 - i, 16) * 8, 8, 8))
    total = oslots[0:8, :]
    for i in range(1, 16):
        total = total + oslots[i * 8:(i + 1) * 8, :]
    obj_ref[...] = total / P_SIZE

    both = rs1.result() + acc[0:PW, :]
    gradient = 0.5 * both - jnp.where(diagonal, 1.0 / own_diag, 0.0)
    stepped = omega_vals - step_size * gradient
    limit = step_size * penalty
    shrunk = stepped - jnp.clip(stepped, -limit, limit)
    panel_ref[...] = jnp.where(diagonal, stepped, shrunk).astype(jnp.bfloat16)

    store_cov.wait()
    for d in started:
        d.wait_send()

    @pl.when(r != c)
    def _():
        desc(tid, own_x, rows(xc, r * piece, piece), d_tr).wait_send()


def per_device(cell_batch, cov_prior, omega_prior):
    piece, width = cell_batch.shape
    any_ = pl.BlockSpec(memory_space=pl.ANY)
    vmem = pl.BlockSpec(memory_space=pltpu.VMEM)
    bf, f32 = jnp.bfloat16, jnp.float32
    cov, panel, obj = pl.pallas_call(
        kernel,
        out_shape=(
            jax.ShapeDtypeStruct((width, width), bf),
            jax.ShapeDtypeStruct((PW, width), bf),
            jax.ShapeDtypeStruct((8, 128), f32),
        ),
        in_specs=[any_] * 3,
        out_specs=(any_, vmem, vmem),
        scratch_shapes=[
            pltpu.VMEM((16 * piece, width), bf),
            pltpu.VMEM((16 * piece, width), bf),
            pltpu.VMEM((16 * PW, width), bf),
            pltpu.VMEM((16 * PW, width), bf),
            pltpu.VMEM((width, width), bf),
            pltpu.VMEM((width, width), bf),
            pltpu.VMEM((width, width), f32),
            pltpu.VMEM((16 * PW, width), f32),
            pltpu.VMEM((PW, width), f32),
            pltpu.VMEM((15 * PW, width), bf),
            pltpu.VMEM((15 * PW, width), bf),
            pltpu.VMEM((15 * PW, width), bf),
            pltpu.VMEM((15 * PW, width), bf),
            pltpu.VMEM((2 * PW, width), f32),
            pltpu.VMEM((128, 128), f32),
            pltpu.VMEM((128, 128), f32),
            pltpu.SemaphoreType.DMA((N_SEM,)),
            pltpu.SemaphoreType.DMA((N_SEM,)),
            pltpu.SemaphoreType.DMA((8,)),
        ],
        compiler_params=pltpu.CompilerParams(
            collective_id=0, has_side_effects=True, vmem_limit_bytes=62 * 1024 * 1024
        ),
    )(cell_batch, cov_prior, omega_prior)
    return cov, panel, obj[0, :PW]


def solution(mesh):
    return jax.shard_map(
        per_device,
        mesh=mesh,
        in_specs=(P("col", "row"), P("row", "col"), P("row", "col")),
        out_specs=(P("row", "col"), P("col", "row"), P("col")),
        check_vma=False,
    )
```

time: 706 us -> 178 us (0.25)
  waiting for transfers between devices: 602 us -> 0 us
  Pallas kernels: 0 us -> 171 us
  blocking collectives: 37.7 us -> 0 us
  matrix products: 27.5 us -> 0 us
  other arithmetic: 14.8 us -> 0 us
  between operations: 13.8 us -> 0.64 us
    reduce_scatter x1 -> x0, waiting for transfers between devices: 220 us -> none  [per_device(): lax.psum_scatter(jnp.concatenate([contract(cov_rows, omega_prior), contra...]
    all_gather x3 -> x0, waiting for transfers between devices: 214 us -> none  [the longest x1 124 us: per_device(): own_slab = lax.all_gather(cell_batch, 'col', axis=0, tiled=True)]
    pallas_call x0 -> x1, Pallas kernels: none -> 171 us  [per_device(): pl.pallas_call(kernel, out_shape=(jax.ShapeDtypeStruct((width, width), bf...]
    psum x1 -> x0, waiting for transfers between devices: 167 us -> none  [broadcast(): return lax.psum(kept, axis)]
    psum x1 -> x0, blocking collectives: 37.7 us -> none  [per_device(): column_objective = lax.psum(quadratic + lasso - logs, 'row') / P_SIZE]
    dot_general x3 -> x0, matrix products: 27.5 us -> none  [the longest x2 16.2 us: contract(): lax.dot_general(left_rows, right_rows, (((1,), (1,)), ((), ())), preferre...]
    concatenate x1 -> x0, other arithmetic: 9.22 us -> none  [per_device(): jnp.concatenate([contract(cov_rows, omega_prior), contract(omega_rows, co...]
  transfers between devices with their start and end apart: 5 -> 0, of which waited for: 5 -> 0; matrix products, arithmetic and copies ran while one was open for 4% -> 0% of each run, Pallas kernels for 0% -> 0%
where the time goes in v1:
time: 178 us; the launch traced here: 177 us
  Pallas kernels  171 us (96%)
  local copies, waits for them, and re-layouts  5.74 us (3%)
    pallas_call x1, Pallas kernels, per_device(): pl.pallas_call(kernel, out_shape=(jax.ShapeDtypeStruct((width, width), bf...  171 us
    unnamed x4, local copies, waits for them, and re-layouts  4.55 us

profile of v1, /device:TPU:32, one launch (start us, length us, event | category | flops | bytes accessed | tf_op | source)
XLA Modules:
  0.0 177.5 jit_solution(822912901274438727)
XLA Ops:
  0.6 171.1 %shard_map.58 = (bf16[1280,1280]{1,0:T(8,128)(2,1)}, bf16[64,1280]{1,0:T(8,128)(2,1)}, f32[8,128]{1,0:T(8,128)}) custom-call(bf16[128,1280]{1,0:T(8,128)(2,1)} %x_hbm.1, bf16[1280,1280]{1,0:T(8,128)(2,1)} %s_hbm.1, bf16[1280,1280]{1,0:T(8,128)(2,1)} %om_hbm.1), custom_call_target="tpu_custom_call" | custom-call | tf_op jit(solution)/shard_map/pallas_call | solution.py:489
  171.7 1.2 slice_bitcast_fusion
  172.9 0.0 copy-start
  172.9 3.9 %copy.8 = bf16[1280,1280]{1,0:T(8,128)(2,1)} copy(bf16[1280,1280]{1,0:T(8,128)(2,1)} %get-tuple-element.12) | data formatting | bytes 6553600
  176.8 0.0 copy-done
  176.8 0.7 copy.9
Async XLA Ops:
  172.9 3.9 %copy-start = (bf16[64,1280]{1,0:T(8,128)(2,1)S(1)}, bf16[64,1280]{1,0:T(8,128)(2,1)}, u32[]{:S(2)}) copy-start(bf16[64,1280]{1,0:T(8,128)(2,1)} %get-tuple-element.13) | copy-start | bytes 491524

commit v2 on v1

--- a/solution.py
+++ b/solution.py
@@ -31,7 +31,7 @@
 
 def kernel(
     x_hbm, s_hbm, om_hbm, cov_hbm, panel_ref, obj_ref,
-    xr, xc, po, pc, om, cv, acc, p1, ov, st2, rv2, st1, rv1, tot, oslots, tr,
+    xr, xc, mid, po, pc, om, cv, acc, p1, ov, st2, rv2, st1, rv1, tot, oslots, tr,
     send_sem, recv_sem, load_sem,
 ):
     r = lax.axis_index("row")
@@ -52,7 +52,16 @@
     d_yp, d_ym = (rowid(y + 1, xh, core), c), (rowid(y - 1, xh, core), c)
     d_xh = (rowid(y, 1 - xh, core), c)
     d_core = (rowid(y, xh, 1 - core), c)
-    d_tr = (c, r)
+
+    shift = lax.rem(lax.div(z + xh, 2), 4)
+    d_mid = (rowid(y + shift, xh, core), c)
+    from_row = rowid(y + 4 - shift, xh, core)
+    to_row = lax.rem(c + from_row - core, 16)
+    d_tr = (to_row, from_row)
+    tr_local = (to_row == r) & (from_row == c)
+    cells = lax.rem(r + 16 - 2 * z, 16)
+    back = lax.rem(lax.div(lax.div(cells, 2) + lax.rem(z, 2), 2), 4)
+    d_src = (rowid(lax.div(z, 2) + back, lax.rem(z, 2), xl), cells)
 
     load_x = pltpu.make_async_copy(x_hbm, rows(xr, c * piece, piece), load_sem.at[0])
     load_x.start()
@@ -73,12 +82,12 @@
     for dev in (d_zp, d_zm, d_xl):
         greet(dev)
 
-    @pl.when(r != c)
-    def _():
-        greet(d_tr)
+    @pl.when(jnp.logical_not(tr_local))
+    def _():
+        greet(d_src)
         pl.semaphore_wait(barrier, 19)
 
-    @pl.when(r == c)
+    @pl.when(tr_local)
     def _():
         pl.semaphore_wait(barrier, 18)
 
@@ -255,41 +264,73 @@
 
     gx = RowGather(xc, piece)
     go_ = RowGather(po, PW)
-    tid = new()
+    tid = new(4)
+    halves = (0, 1)
     load_x.wait()
-    own_x = rows(xr, c * piece, piece)
-
-    @pl.when(r != c)
-    def _():
-        desc(tid, own_x, rows(xc, c * piece, piece), d_tr).start()
-
-    @pl.when(r == c)
-    def _():
-        pltpu.make_async_copy(own_x, rows(xc, c * piece, piece), load_sem.at[4]).start()
+
+    def to_mid(h):
+        return desc(tid + h, rows(xr, c * piece + h * ph, ph), rows(mid, h * ph, ph), d_mid)
+
+    def to_slot(h):
+        return desc(tid + 2 + h, rows(mid, h * ph, ph), rows(xc, to_row * piece + h * ph, ph), d_tr)
+
+    def keep():
+        return pltpu.make_async_copy(rows(xr, c * piece, piece), mid, load_sem.at[4])
+
+    def land():
+        return pltpu.make_async_copy(mid, rows(xc, r * piece, piece), load_sem.at[7])
+
+    @pl.when(shift != 0)
+    def _():
+        for h in halves:
+            to_mid(h).start()
+
+    @pl.when(shift == 0)
+    def _():
+        keep().start()
 
     col0()
     load_po.wait()
     go_.s0()
+
+    @pl.when(shift == 0)
+    def _():
+        keep().wait()
+
+    for h in halves:
+        @pl.when(shift != 0)
+        def _(h=h):
+            to_mid(h).wait_recv()
+
+        @pl.when(jnp.logical_not(tr_local))
+        def _(h=h):
+            to_slot(h).start()
+
+    @pl.when(tr_local)
+    def _():
+        land().start()
+
     acc[...] = jnp.zeros_like(acc)
     col1()
-
-    @pl.when(r != c)
-    def _():
-        desc(tid, own_x, rows(xc, r * piece, piece), d_tr).wait_recv()
-
-    @pl.when(r == c)
-    def _():
-        pltpu.make_async_copy(own_x, rows(xc, r * piece, piece), load_sem.at[4]).wait()
+    go_.s1()
+    colp(1)
+    colq(1)
+    go_.s2()
+
+    @pl.when(jnp.logical_not(tr_local))
+    def _():
+        for h in halves:
+            desc(tid + 2 + h, rows(mid, h * ph, ph), rows(xc, r * piece + h * ph, ph), d_tr).wait_recv()
+
+    @pl.when(tr_local)
+    def _():
+        land().wait()
 
     gx.s0()
-    go_.s1()
+    go_.s3()
     gx.s1()
-    colp(1)
-    go_.s2()
-    colq(1)
-    go_.s3()
+    colp(2)
     gx.s2()
-    colp(2)
     go_.s4()
     colq(2)
     gx.s3()
@@ -307,11 +348,12 @@
         def body(i, carry):
             j = lax.rem(z + lo + i + 8, 8)
             k0 = pl.multiple_of(j * 2 * piece, 2 * piece)
+            s0 = pl.multiple_of(lax.rem(j + z, 8) * 2 * piece, 2 * piece)
 
             def inner(m, carry2):
                 m0 = pl.multiple_of(m * tile, tile)
                 a = xr[pl.ds(k0, 2 * piece), pl.ds(m0, tile)]
-                b = xc[pl.ds(k0, 2 * piece), :]
+                b = xc[pl.ds(s0, 2 * piece), :]
                 acc[pl.ds(m0, tile), :] += lax.dot_general(
                     a, b, (((0,), (0,)), ((), ())), preferred_element_type=jnp.float32
                 )
@@ -476,9 +518,15 @@
     for d in started:
         d.wait_send()
 
-    @pl.when(r != c)
-    def _():
-        desc(tid, own_x, rows(xc, r * piece, piece), d_tr).wait_send()
+    @pl.when(shift != 0)
+    def _():
+        for h in halves:
+            to_mid(h).wait_send()
+
+    @pl.when(jnp.logical_not(tr_local))
+    def _():
+        for h in halves:
+            to_slot(h).wait_send()
 
 
 def per_device(cell_batch, cov_prior, omega_prior):
@@ -498,6 +546,7 @@
         scratch_shapes=[
             pltpu.VMEM((16 * piece, width), bf),
             pltpu.VMEM((16 * piece, width), bf),
+            pltpu.VMEM((piece, width), bf),
             pltpu.VMEM((16 * PW, width), bf),
             pltpu.VMEM((16 * PW, width), bf),
             pltpu.VMEM((width, width), bf),

time: 178 us -> 163 us (0.916)
  Pallas kernels: 171 us -> 156 us
    pallas_call x1, Pallas kernels: 171 us -> 156 us  [per_device(): pl.pallas_call(kernel, out_shape=(jax.ShapeDtypeStruct((width, width), bf...]
where the time goes in v2:
time: 163 us; the launch traced here: 162 us
  Pallas kernels  156 us (96%)
  local copies, waits for them, and re-layouts  5.74 us (4%)
    pallas_call x1, Pallas kernels, per_device(): pl.pallas_call(kernel, out_shape=(jax.ShapeDtypeStruct((width, width), bf...  156 us
    unnamed x4, local copies, waits for them, and re-layouts  4.55 us

profile of v2, /device:TPU:32, one launch (start us, length us, event | category | flops | bytes accessed | tf_op | source)
XLA Modules:
  0.0 162.2 jit_solution(756512679104297446)
XLA Ops:
  0.6 155.8 %shard_map.58 = (bf16[1280,1280]{1,0:T(8,128)(2,1)}, bf16[64,1280]{1,0:T(8,128)(2,1)}, f32[8,128]{1,0:T(8,128)}) custom-call(bf16[128,1280]{1,0:T(8,128)(2,1)} %x_hbm.1, bf16[1280,1280]{1,0:T(8,128)(2,1)} %s_hbm.1, bf16[1280,1280]{1,0:T(8,128)(2,1)} %om_hbm.1), custom_call_target="tpu_custom_call" | custom-call | tf_op jit(solution)/shard_map/pallas_call | solution.py:537
  156.5 1.2 slice_bitcast_fusion
  157.7 0.0 copy-start
  157.7 3.9 %copy.8 = bf16[1280,1280]{1,0:T(8,128)(2,1)} copy(bf16[1280,1280]{1,0:T(8,128)(2,1)} %get-tuple-element.12) | data formatting | bytes 6553600
  161.5 0.0 copy-done
  161.5 0.7 copy.9
Async XLA Ops:
  157.7 3.9 %copy-start = (bf16[64,1280]{1,0:T(8,128)(2,1)S(1)}, bf16[64,1280]{1,0:T(8,128)(2,1)}, u32[]{:S(2)}) copy-start(bf16[64,1280]{1,0:T(8,128)(2,1)} %get-tuple-element.13) | copy-start | bytes 491524

commit v3 on v2

--- a/solution.py
+++ b/solution.py
@@ -398,13 +398,14 @@
     gc.s0()
     lax.fori_loop(2, width // 128 - 1, fin_body, 0)
 
-    def product(dst, left, right):
-        def body(m, carry):
-            m0 = pl.multiple_of(m * tile, tile)
-            dst[pl.ds(m0, tile), :] = nt(left[pl.ds(m0, tile), :], right[...])
+    def product(dst, left, right, d):
+        def body(i, carry):
+            zz = lax.rem(z + 8 + d * (1 - 2 * i), 8)
+            m0 = pl.multiple_of(zz * 2 * PW, 2 * PW)
+            dst[pl.ds(m0, 2 * PW), :] = nt(left[pl.ds(m0, 2 * PW), :], right[...])
             return carry
 
-        lax.fori_loop(0, 16 * PW // tile, body, 0)
+        lax.fori_loop(0, 1 if d in (0, 4) else 2, body, 0)
 
     class Scatter:
         def __init__(self, src, st, rv):
@@ -455,27 +456,32 @@
         def result(self):
             return tot[pl.ds(pl.multiple_of(xl * PW, PW), PW), :] + self.got(("x", 0, 0))
 
-    product(acc, po, cv)
     store_cov = pltpu.make_async_copy(cv, cov_hbm, load_sem.at[6])
     store_cov.start()
     rs2 = Scatter(acc, st2, rv2)
     rs1 = Scatter(p1, st1, rv1)
+    product(acc, po, cv, 4)
     rs2.step(0)
+    product(acc, po, cv, 3)
     gc.s1()
     rs2.step(1)
+    product(acc, po, cv, 2)
     gc.s2()
     rs2.step(2)
     gc.s3()
+    product(acc, po, cv, 1)
     rs2.step(3)
     gc.s4()
+    product(acc, po, cv, 0)
     rs2.close()
     gc.s5()
 
-    product(p1, pc, om)
+    product(p1, pc, om, 4)
+    rs1.step(0)
+    product(p1, pc, om, 3)
+    rs1.step(1)
     second_sum = rs2.result()
     acc[0:PW, :] = second_sum
-    rs1.step(0)
-    rs1.step(1)
 
     omega_vals = ov[...]
     lane = lax.broadcasted_iota(jnp.int32, (PW, width), 1)
@@ -494,11 +500,14 @@
     oslots[pl.ds(pl.multiple_of(r * 8, 8), 8), :] = jnp.broadcast_to(line, (8, 128))
     oid = new(16)
 
+    product(p1, pc, om, 2)
     rs1.step(2)
     mine = rows(oslots, r * 8, 8, 8)
     for i in range(1, 16):
         send(oid + i, mine, mine, (lax.rem(r + i, 16), c))
+    product(p1, pc, om, 1)
     rs1.step(3)
+    product(p1, pc, om, 0)
     rs1.close()
     for i in range(1, 16):
         arrived(oid + i, rows(oslots, lax.rem(r + 16 - i, 16) * 8, 8, 8))

time: 163 us -> 157 us (0.963)
  Pallas kernels: 156 us -> 150 us
    pallas_call x1, Pallas kernels: 156 us -> 150 us  [per_device(): pl.pallas_call(kernel, out_shape=(jax.ShapeDtypeStruct((width, width), bf...]
where the time goes in v3:
time: 157 us; the launch traced here: 156 us
  Pallas kernels  150 us (96%)
  local copies, waits for them, and re-layouts  5.74 us (4%)
    pallas_call x1, Pallas kernels, per_device(): pl.pallas_call(kernel, out_shape=(jax.ShapeDtypeStruct((width, width), bf...  150 us
    unnamed x4, local copies, waits for them, and re-layouts  4.55 us

profile of v3, /device:TPU:32, one launch (start us, length us, event | category | flops | bytes accessed | tf_op | source)
XLA Modules:
  0.0 156.1 jit_solution(9471581544102552782)
XLA Ops:
  0.6 149.7 %shard_map.58 = (bf16[1280,1280]{1,0:T(8,128)(2,1)}, bf16[64,1280]{1,0:T(8,128)(2,1)}, f32[8,128]{1,0:T(8,128)}) custom-call(bf16[128,1280]{1,0:T(8,128)(2,1)} %x_hbm.1, bf16[1280,1280]{1,0:T(8,128)(2,1)} %s_hbm.1, bf16[1280,1280]{1,0:T(8,128)(2,1)} %om_hbm.1), custom_call_target="tpu_custom_call" | custom-call | tf_op jit(solution)/shard_map/pallas_call | solution.py:546
  150.4 1.2 slice_bitcast_fusion
  151.6 0.0 copy-start
  151.6 3.9 %copy.8 = bf16[1280,1280]{1,0:T(8,128)(2,1)} copy(bf16[1280,1280]{1,0:T(8,128)(2,1)} %get-tuple-element.12) | data formatting | bytes 6553600
  155.4 0.0 copy-done
  155.4 0.7 copy.9
Async XLA Ops:
  151.6 3.9 %copy-start = (bf16[64,1280]{1,0:T(8,128)(2,1)S(1)}, bf16[64,1280]{1,0:T(8,128)(2,1)}, u32[]{:S(2)}) copy-start(bf16[64,1280]{1,0:T(8,128)(2,1)} %get-tuple-element.13) | copy-start | bytes 491524
